TPU v7x, 32 devices: a whole 2x2x4 slice. The times are simulated.
32 devices in a mesh: replica: 8 (over z, x), tensor: 4 (over y, core).
Axes of the slice: x: 2, y: 2, z: 4, core: 2. Of those that a mesh axis runs over, the one named last changes fastest.
Arguments:
- hidden: bfloat16 [256, 8192], P('replica'), may hold values from -16 to 16
- q_weight: bfloat16 [8192, 4096], P(None, 'tensor'), may hold values from -0.0625 to 0.0625
- q_gain: float32 [128], replicated, may hold values from 0.1 to 1.9
- o_weight: bfloat16 [4096, 8192], P('tensor'), may hold values from -0.125 to 0.125
- attn_gate: float32 [1], replicated, may hold values from 0.5 to 1.5
- key_codes: bfloat16 [64, 128, 1024], P('replica', 'tensor'), may hold values from -96 to 96
- value_codes: bfloat16 [64, 128, 1024], P('replica', 'tensor'), may hold values from -96 to 96
- key_scales: bfloat16 [64, 4, 8], P('replica', 'tensor'), may hold values from 0.02 to 8
- value_scales: bfloat16 [64, 4, 8], P('replica', 'tensor'), may hold values from 0.019897461 to 0.119628906
- lengths: int32 [64], P('replica'), may hold values from 32 to 128
- dest_replica: int32 [8, 6], replicated, may hold values from 0 to 7, as said below
- move_slot: int32 [8, 6], P('replica'), may hold values from 0 to 7, as said below
Outputs:
- mixed: bfloat16 [256, 8192], P('replica', 'tensor')
- new_keys: bfloat16 [64, 128, 1024], P('replica', 'tensor')
- new_values: bfloat16 [64, 128, 1024], P('replica', 'tensor')
- new_key_scales: bfloat16 [64, 4, 8], P('replica', 'tensor')
- new_value_scales: bfloat16 [64, 4, 8], P('replica', 'tensor')
Inputs may be any that keep to these rules, and one draw needn't show every extreme that they name: For each j the column dest_replica[:, j] names every replica once, so each replica receives exactly 6 requests, at most one from each replica; a request may stay on its own replica. `move_slot`: the 6 slots of one replica are different.
All inputs are finite; a program needn't handle non-finite values.
Results may differ from a plain program's by a relative error of at most 0.0065.
Values may be sent and summed in bfloat16 or wider, within the bound.
A program may use at most 64 MiB of HBM per device.

v0:
```python
import jax
import jax.numpy as jnp
from jax import lax
from jax.sharding import PartitionSpec as P

NEGATIVE = -1e30
EPSILON = 1e-06


def merged(array, axis, combine):
    everything = jax.tree.map(lambda part: lax.all_gather(part, axis), array)
    first = jax.tree.map(lambda part: part[0], everything)

    def hop(k, so_far):
        return combine(so_far, jax.tree.map(lambda part: part[k], everything))

    return lax.fori_loop(1, lax.axis_size(axis), hop, first)


def softmax_merge(first, second):
    top = jnp.maximum(first[0], second[0])
    left = jnp.exp(first[0] - top)
    right = jnp.exp(second[0] - top)
    total = first[1] * left + second[1] * right
    summed = first[2] * left[..., None] + second[2] * right[..., None]
    return (top, total, summed)


def outgoing(send_table, codes):
    flat = codes.reshape(codes.shape[0], -1)
    moved = jnp.dot(send_table, flat, preferred_element_type=jnp.float32)
    return moved.astype(jnp.bfloat16).reshape((send_table.shape[0],) + codes.shape[1:])


def incoming(select, keep, received, codes):
    flat = received.reshape(received.shape[0], -1)
    placed = jnp.dot(select, flat, preferred_element_type=jnp.float32).astype(jnp.bfloat16)
    former = codes.reshape(codes.shape[0], -1)
    return jnp.where(keep[:, None], former, placed).reshape(codes.shape)


def attend(
    hidden,
    q_weight,
    q_gain,
    o_weight,
    attn_gate,
    key_codes,
    value_codes,
    key_scales,
    value_scales,
    lengths,
):
    rank = lax.axis_index("tensor")
    held, span, kv_width = key_codes.shape
    kv_heads = key_scales.shape[2]
    head_dim = kv_width // kv_heads
    rows = hidden.shape[0]
    drafts = rows // held
    local_heads = q_weight.shape[1] // head_dim
    projected = jnp.dot(hidden, q_weight, preferred_element_type=jnp.float32).reshape(
        rows, local_heads, head_dim
    )
    projected = projected * lax.rsqrt(
        jnp.mean(projected * projected, axis=-1, keepdims=True) + EPSILON
    )
    query = (projected * q_gain * head_dim ** (-0.5)).astype(jnp.bfloat16)
    every_head = lax.all_gather(query, "tensor", axis=1, tiled=True)
    heads = every_head.shape[1]
    grouped = every_head.reshape(held, drafts, kv_heads, heads // kv_heads, head_dim)
    keys = key_codes.reshape(held, span, kv_heads, head_dim)
    values = value_codes.reshape(held, span, kv_heads, head_dim)
    scores = jnp.einsum("rsngd,rtnd->rsngt", grouped, keys, preferred_element_type=jnp.float32)
    scores = scores * key_scales[:, 0, :].astype(jnp.float32)[:, None, :, None, None]
    position = rank * span + jnp.arange(span, dtype=jnp.int32)
    valid = (position[None, :] < lengths[:, None])[:, None, None, None, :]
    block_max = jnp.max(jnp.where(valid, scores, NEGATIVE), axis=-1)
    weights = jnp.where(valid, jnp.exp(scores - block_max[..., None]), 0.0)
    block_sum = jnp.sum(weights, axis=-1)
    block_out = jnp.einsum(
        "rsngt,rtnd->rsngd",
        weights.astype(jnp.bfloat16),
        values,
        preferred_element_type=jnp.float32,
    )
    block_out = block_out * value_scales[:, 0, :].astype(jnp.float32)[:, None, :, None, None]
    partial_value = (
        block_max.reshape(rows, heads),
        block_sum.reshape(rows, heads),
        block_out.reshape(rows, heads, head_dim),
    )
    top, total, summed = merged(partial_value, "tensor", softmax_merge)
    total = lax.dynamic_slice_in_dim(total, rank * local_heads, local_heads, 1)
    summed = lax.dynamic_slice_in_dim(summed, rank * local_heads, local_heads, 1)
    attended = (
        (summed / total[..., None]).astype(jnp.bfloat16).reshape(rows, local_heads * head_dim)
    )
    terms = jnp.dot(attended, o_weight, preferred_element_type=jnp.float32)
    shares = lax.psum_scatter(terms, "tensor", scatter_dimension=1, tiled=True)
    width = shares.shape[1]
    residual = lax.dynamic_slice_in_dim(hidden, rank * width, width, 1).astype(jnp.float32)
    return (residual + jnp.tanh(attn_gate[0]) * shares).astype(jnp.bfloat16)


def local(
    hidden,
    q_weight,
    q_gain,
    o_weight,
    attn_gate,
    key_codes,
    value_codes,
    key_scales,
    value_scales,
    lengths,
    dest_replica,
    move_slot,
):
    replicas = lax.axis_size("replica")
    here = lax.axis_index("replica")
    held = key_codes.shape[0]
    slots = move_slot[0]
    own_dest = lax.dynamic_index_in_dim(dest_replica, here, 0, keepdims=False)
    replica_ids = jnp.arange(replicas, dtype=jnp.int32)
    slot_ids = jnp.arange(held, dtype=jnp.int32)
    slot_match = slots[:, None] == slot_ids[None, :]
    send_table = jnp.any(
        (own_dest[:, None, None] == replica_ids[None, :, None]) & slot_match[:, None, :], axis=0
    ).astype(jnp.bfloat16)
    arrive = dest_replica == here
    select = jnp.any(slot_match.T[:, None, :] & arrive[None, :, :], axis=2).astype(jnp.bfloat16)
    keep = jnp.logical_not(jnp.any(slot_match, axis=0))
    received = (
        lax.all_to_all(
            outgoing(send_table, key_codes), "replica", split_axis=0, concat_axis=0, tiled=True
        ),
        lax.all_to_all(
            outgoing(send_table, value_codes), "replica", split_axis=0, concat_axis=0, tiled=True
        ),
        lax.all_to_all(
            outgoing(send_table, key_scales), "replica", split_axis=0, concat_axis=0, tiled=True
        ),
        lax.all_to_all(
            outgoing(send_table, value_scales), "replica", split_axis=0, concat_axis=0, tiled=True
        ),
    )
    new_keys = incoming(select, keep, received[0], key_codes)
    new_values = incoming(select, keep, received[1], value_codes)
    new_key_scales = incoming(select, keep, received[2], key_scales)
    new_value_scales = incoming(select, keep, received[3], value_scales)
    mixed = attend(
        hidden,
        q_weight,
        q_gain,
        o_weight,
        attn_gate,
        key_codes,
        value_codes,
        key_scales,
        value_scales,
        lengths,
    )
    return (mixed, new_keys, new_values, new_key_scales, new_value_scales)


def solution(mesh):
    return jax.shard_map(
        local,
        mesh=mesh,
        in_specs=(
            P("replica", None),
            P(None, "tensor"),
            P(),
            P("tensor", None),
            P(),
            P("replica", "tensor", None),
            P("replica", "tensor", None),
            P("replica", "tensor", None),
            P("replica", "tensor", None),
            P("replica"),
            P(),
            P("replica", None),
        ),
        out_specs=(
            P("replica", "tensor"),
            P("replica", "tensor", None),
            P("replica", "tensor", None),
            P("replica", "tensor", None),
            P("replica", "tensor", None),
        ),
        check_vma=False,
    )
```

profile of v0, /device:TPU:0, one launch (start us, length us, event | category | flops | bytes accessed | tf_op | source)
XLA Modules:
  0.0 117.9 jit_solution(6029297869704458706)
XLA Ops:
  7.3 0.7 bitcast_convert_fusion.1
  8.0 1.1 copy.75
  9.2 9.0 %convolution_bitcast_fusion = f32[4,8,8,128]{3,1,2,0:T(8,128)S(1)} fusion(bf16[32,8192]{1,0:T(8,128)(2,1)} %param.14, bf16[8192,1024]{1,0:T(8,128)(2,1)} %param.15), kind=kOutput, calls=%fused_computation.18 | convolution fusion | flops 536870912 | bytes 17432576 | tf_op jit(solution)/shard_map/dot_general | solution.py:61
  18.5 7.3 %all_gather.12 = bf16[32,32,128]{2,1,0:T(8,128)(2,1)S(1)} all-gather(bf16[32,8,128]{2,1,0:T(8,128)(2,1)S(1)} %multiply_convert_fusion), channel_id=1, replica_groups=mesh['replica'=8,'tensor'=4] {'tensor'}, dimensions={1}, use_global_device_ids=true | all-gather | bytes 327680 | tf_op jit(solution)/shard_map/all_gather | solution.py:68
  27.1 0.9 copy.58
  28.4 0.6 copy.62
  29.0 5.8 %all-to-all-start.2 = ((bf16[8,1,8]{2,1,0:T(2,128)(2,1)}), bf16[8,1,8]{2,1,0:T(2,128)(2,1)S(1)}, u32[]{:S(2)}, u32[]{:S(2)}) async-start(bf16[8,1,8]{2,1,0:T(2,128)(2,1)} %copy.62), calls=%async_computation.3 | async-start | bytes 8192 | tf_op jit(solution)/shard_map/all_to_all | solution.py:140
  35.0 0.8 fusion.16
  36.5 1.1 copy.60
  37.7 0.6 copy.63
  38.3 5.7 %all_gather.13 = f32[4,32,32]{2,1,0:T(8,128)S(1)} all-gather(f32[1,32,32]{2,1,0:T(8,128)S(1)} %all_gather_reshape.9), channel_id=1, replica_groups=mesh['replica'=8,'tensor'=4] {'tensor'}, dimensions={0}, use_global_device_ids=true | all-gather | bytes 20480 | tf_op jit(solution)/shard_map/all_gather | solution.py:11
  44.0 5.6 %all_gather.14 = f32[4,32,32]{2,1,0:T(8,128)S(1)} all-gather(f32[1,32,32]{2,1,0:T(8,128)S(1)} %all_gather_reshape.10), channel_id=1, replica_groups=mesh['replica'=8,'tensor'=4] {'tensor'}, dimensions={0}, use_global_device_ids=true | all-gather | bytes 20480 | tf_op jit(solution)/shard_map/all_gather | solution.py:11
  49.6 3.2 %all-gather.2.cloned.1.call-done = f32[4,32,32,128]{3,2,1,0:T(8,128)} async-done(((f32[1,32,32,128]{3,2,1,0:T(8,128)}), f32[4,32,32,128]{3,2,1,0:T(8,128)}) %all-gather.2.cloned.1.call-update) | async-done | bytes 2097168 | tf_op jit(solution)/shard_map/all_gather | solution.py:11
  52.8 1.1 slice_bitcast_fusion
  53.9 4.8 %while.19 = (s32[]{:T(128)}, f32[32,32]{1,0:T(8,128)S(1)}, f32[32,32]{1,0:T(8,128)S(1)}, f32[32,32,128]{2,1,0:T(8,128)S(1)}, f32[4,32,32]{2,1,0:T(8,128)S(1)}, /...) while((s32[]{:T(128)}, f32[32,32]{1,0:T(8,128)S(1)}, ...), condition=%wide.region_4.5_spmd, body=%wide.region_3.4_spmd.sunk | while | flops 399365 | bytes 1613975 | solution.py:17
  53.9 1.5 %fusion.53 = f32[32,32,128]{2,1,0:T(8,128)S(1)} fusion(f32[4,32,32,128]{3,2,1,0:T(8,128)} %get-tuple-element.309, s32[]{:T(128)S(6)} %select_n.69, f32[32,32,128]{2,1,0:T(8,128)S(1)} %get-tuple-element.296, f32[32,32]{1,0:T(8,128)S(1)} %get-tuple-element.281, f32[32,32]{1,0:T(8,128)S(1)} %get-tuple-element.282), kind=kLoop, calls=%fused_computation.1.clone.1 | loop fusion | flops 393216 | bytes 1581060 | tf_op jit(solution)/shard_map/while/body/eval_jaxpr/add | solution.py:25
  55.5 1.5 %fusion.53 = f32[32,32,128]{2,1,0:T(8,128)S(1)} fusion(f32[4,32,32,128]{3,2,1,0:T(8,128)} %get-tuple-element.309, s32[]{:T(128)S(6)} %select_n.69, f32[32,32,128]{2,1,0:T(8,128)S(1)} %get-tuple-element.296, f32[32,32]{1,0:T(8,128)S(1)} %get-tuple-element.281, f32[32,32]{1,0:T(8,128)S(1)} %get-tuple-element.282), kind=kLoop, calls=%fused_computation.1.clone.1 | loop fusion | flops 393216 | bytes 1581060 | tf_op jit(solution)/shard_map/while/body/eval_jaxpr/add | solution.py:25
  57.1 1.5 %fusion.53 = f32[32,32,128]{2,1,0:T(8,128)S(1)} fusion(f32[4,32,32,128]{3,2,1,0:T(8,128)} %get-tuple-element.309, s32[]{:T(128)S(6)} %select_n.69, f32[32,32,128]{2,1,0:T(8,128)S(1)} %get-tuple-element.296, f32[32,32]{1,0:T(8,128)S(1)} %get-tuple-element.281, f32[32,32]{1,0:T(8,128)S(1)} %get-tuple-element.282), kind=kLoop, calls=%fused_computation.1.clone.1 | loop fusion | flops 393216 | bytes 1581060 | tf_op jit(solution)/shard_map/while/body/eval_jaxpr/add | solution.py:25
  58.7 5.5 %all-to-all-start.3 = ((bf16[8,1,8]{2,1,0:T(2,128)(2,1)}), bf16[8,1,8]{2,1,0:T(2,128)(2,1)S(1)}, u32[]{:S(2)}, u32[]{:S(2)}) async-start(bf16[8,1,8]{2,1,0:T(2,128)(2,1)} %copy.63), calls=%async_computation.4 | async-start | bytes 8192 | tf_op jit(solution)/shard_map/all_to_all | solution.py:143
  64.4 6.4 %all-to-all-done.3 = bf16[8,1,8]{2,1,0:T(2,128)(2,1)S(1)} async-done(((bf16[8,1,8]{2,1,0:T(2,128)(2,1)}), bf16[8,1,8]{2,1,0:T(2,128)(2,1)S(1)}, u32[]{:S(2)}, u32[]{:S(2)}) %all-to-all-start.3) | async-done | bytes 160 | tf_op jit(solution)/shard_map/all_to_all | solution.py:143
  70.7 3.5 %all-to-all-start = ((bf16[8,32,1024]{2,1,0:T(8,128)(2,1)}), bf16[8,32,1024]{2,1,0:T(8,128)(2,1)S(1)}, u32[]{:S(2)}, u32[]{:S(2)}) async-start(bf16[8,32,1024]{2,1,0:T(8,128)(2,1)} %copy.60), calls=%async_computation.1 | async-start | bytes 1048576 | tf_op jit(solution)/shard_map/all_to_all | solution.py:134
  74.3 9.7 %fusion.22 = f32[32,8192]{1,0:T(8,128)} fusion(bf16[1024,8192]{1,0:T(8,128)(2,1)} %param.17, bf16[4,8,8,128]{3,2,1,0:T(8,128)(2,1)S(1)} %bitcast.134), kind=kOutput, calls=%fused_computation.46 | convolution fusion | flops 536870912 | bytes 17891328 | tf_op jit(solution)/shard_map/dot_general | solution.py:98
  84.6 1.1 copy.61
  85.7 2.2 %all-to-all-done = bf16[8,32,1024]{2,1,0:T(8,128)(2,1)S(1)} async-done(((bf16[8,32,1024]{2,1,0:T(8,128)(2,1)}), bf16[8,32,1024]{2,1,0:T(8,128)(2,1)S(1)}, u32[]{:S(2)}, u32[]{:S(2)}) %all-to-all-start) | async-done | bytes 524320 | tf_op jit(solution)/shard_map/all_to_all | solution.py:134
  87.9 3.7 %all-to-all-start.1 = ((bf16[8,32,1024]{2,1,0:T(8,128)(2,1)}), bf16[8,32,1024]{2,1,0:T(8,128)(2,1)S(1)}, u32[]{:S(2)}, u32[]{:S(2)}) async-start(bf16[8,32,1024]{2,1,0:T(8,128)(2,1)} %copy.61), calls=%async_computation.2 | async-start | bytes 1048576 | tf_op jit(solution)/shard_map/all_to_all | solution.py:137
  92.6 0.7 fusion.10
  93.3 0.7 fusion.12
  94.6 1.1 copy.64
  95.7 9.7 %all-to-all-done.1 = bf16[8,32,1024]{2,1,0:T(8,128)(2,1)S(1)} async-done(((bf16[8,32,1024]{2,1,0:T(8,128)(2,1)}), bf16[8,32,1024]{2,1,0:T(8,128)(2,1)S(1)}, u32[]{:S(2)}, u32[]{:S(2)}) %all-to-all-start.1) | async-done | bytes 524320 | tf_op jit(solution)/shard_map/all_to_all | solution.py:137
  106.0 1.1 copy.65
  107.1 2.4 %reduce-scatter.2.cloned.1.call-done = f32[32,2048]{1,0:T(8,128)} async-done(((f32[32,8192]{1,0:T(8,128)}), f32[32,2048]{1,0:T(8,128)}) %reduce-scatter.2.cloned.1.call-update) | async-done | bytes 262160 | tf_op jit(solution)/shard_map/reduce_scatter | solution.py:99
  109.4 1.7 %add_convert_fusion = bf16[32,2048]{1,0:T(8,128)(2,1)} fusion(f32[32,2048]{1,0:T(8,128)} %reduce-scatter.2.cloned.1.call-done, f32[]{:T(128)} %bitcast.3, bf16[32,8192]{1,0:T(8,128)(2,1)} %param.14, s32[]{:T(128)S(6)} %select_n.44), kind=kLoop, calls=%fused_computation.39 | loop fusion | flops 262144 | bytes 524296 | tf_op jit(solution)/shard_map/convert_element_type | solution.py:102
  (62 shorter events, 5.2 us)
Async XLA Ops:
  7.2 11.2 %copy-start.5 = (f32[128]{0:T(128)S(1)}, f32[128]{0:T(128)}, u32[]{:S(2)}) copy-start(f32[128]{0:T(128)} %param.16) | copy-start | bytes 1540
  7.2 18.6 %copy-start.1 = (bf16[8,32,1024]{2,1,0:T(8,128)(2,1)S(1)}, bf16[8,32,1024]{2,1,0:T(8,128)(2,1)}, u32[]{:S(2)}) copy-start(bf16[8,32,1024]{2,1,0:T(8,128)(2,1)} %param.20) | copy-start | bytes 1572868
  7.2 18.7 %copy-start.3 = (bf16[8,1,8]{2,0,1:T(8,128)(2,1)S(1)}, bf16[8,1,8]{2,0,1:T(8,128)(2,1)}, u32[]{:S(2)}) copy-start(bf16[8,1,8]{2,0,1:T(8,128)(2,1)} %param.22) | copy-start | bytes 388
  7.2 18.8 %copy-start.7 = (s32[8]{0:T(128)S(1)}, s32[8]{0:T(128)}, u32[]{:S(2)}) copy-start(s32[8]{0:T(128)} %param.23) | copy-start | bytes 100
  7.2 45.6 %all-gather.2.cloned.1.call-start = ((), (), s32[]{:S(2)}) async-start(), calls=%async_computation.5 | async-start | bytes 2621440 | tf_op jit(solution)/shard_map/all_gather | solution.py:11
  9.2 18.9 %copy-start.4 = (s32[8,6]{1,0:T(8,128)S(1)}, s32[8,6]{1,0:T(8,128)}, u32[]{:S(2)}) copy-start(s32[8,6]{1,0:T(8,128)} %param.24) | copy-start | bytes 580
  9.2 18.9 %copy-start.6 = (s32[1,6]{1,0:T(1,128)S(1)}, s32[1,6]{1,0:T(1,128)}, u32[]{:S(2)}) copy-start(s32[1,6]{1,0:T(1,128)} %param.25) | copy-start | bytes 76
  9.2 19.1 %copy-start.2 = (bf16[8,1,8]{2,0,1:T(8,128)(2,1)S(1)}, bf16[8,1,8]{2,0,1:T(8,128)(2,1)}, u32[]{:S(2)}) copy-start(bf16[8,1,8]{2,0,1:T(8,128)(2,1)} %param.21) | copy-start | bytes 388
  9.2 26.7 %copy-start = (bf16[8,32,1024]{2,1,0:T(8,128)(2,1)S(1)}, bf16[8,32,1024]{2,1,0:T(8,128)(2,1)}, u32[]{:S(2)}) copy-start(bf16[8,32,1024]{2,1,0:T(8,128)(2,1)} %param.19) | copy-start | bytes 1572868
  29.0 29.7 %all-to-all-start.2 = ((bf16[8,1,8]{2,1,0:T(2,128)(2,1)}), bf16[8,1,8]{2,1,0:T(2,128)(2,1)S(1)}, u32[]{:S(2)}, u32[]{:S(2)}) async-start(bf16[8,1,8]{2,1,0:T(2,128)(2,1)} %copy.62), calls=%async_computation.3 | async-start | bytes 8192 | tf_op jit(solution)/shard_map/all_to_all | solution.py:140
  58.7 12.0 %all-to-all-start.3 = ((bf16[8,1,8]{2,1,0:T(2,128)(2,1)}), bf16[8,1,8]{2,1,0:T(2,128)(2,1)S(1)}, u32[]{:S(2)}, u32[]{:S(2)}) async-start(bf16[8,1,8]{2,1,0:T(2,128)(2,1)} %copy.63), calls=%async_computation.4 | async-start | bytes 8192 | tf_op jit(solution)/shard_map/all_to_all | solution.py:143
  70.7 17.2 %all-to-all-start = ((bf16[8,32,1024]{2,1,0:T(8,128)(2,1)}), bf16[8,32,1024]{2,1,0:T(8,128)(2,1)S(1)}, u32[]{:S(2)}, u32[]{:S(2)}) async-start(bf16[8,32,1024]{2,1,0:T(8,128)(2,1)} %copy.60), calls=%async_computation.1 | async-start | bytes 1048576 | tf_op jit(solution)/shard_map/all_to_all | solution.py:134
  74.2 35.2 %reduce-scatter.2.cloned.1.call-start = ((), (), s32[]{:S(2)}) async-start(), calls=%async_computation.6 | async-start | bytes 1310720 | tf_op jit(solution)/shard_map/reduce_scatter | solution.py:99
  87.9 17.5 %all-to-all-start.1 = ((bf16[8,32,1024]{2,1,0:T(8,128)(2,1)}), bf16[8,32,1024]{2,1,0:T(8,128)(2,1)S(1)}, u32[]{:S(2)}, u32[]{:S(2)}) async-start(bf16[8,32,1024]{2,1,0:T(8,128)(2,1)} %copy.61), calls=%async_computation.2 | async-start | bytes 1048576 | tf_op jit(solution)/shard_map/all_to_all | solution.py:137
Sparse Core Ops, SparseCore 0:
  28.2 24.5 all-gather.1
  84.2 25.1 reduce-scatter.1
where the time goes:
time: 119 us; the launch traced here: 118 us
  waiting for transfers between devices  23.9 us (20%)
  matrix products  22.6 us (19%)
  starting transfers between devices  18.6 us (16%)
  blocking collectives  18.5 us (16%)
  between operations  15.1 us (13%)
  local copies, waits for them, and re-layouts  10.5 us (9%)
  other arithmetic  8.61 us (7%)
    all_gather x2, blocking collectives, merged(): everything = jax.tree.map(lambda part: lax.all_gather(part, axis), array)  11.3 us
    all_to_all x1, waiting for transfers between devices, local(): lax.all_to_all(outgoing(send_table, value_codes), 'replica', split_axis=0...  9.74 us
    dot_general x1, matrix products, attend(): terms = jnp.dot(attended, o_weight, preferred_element_type=jnp.float32)  9.73 us
    dot_general x1, matrix products, attend(): jnp.dot(hidden, q_weight, preferred_element_type=jnp.float32)  8.98 us
    all_gather x1, blocking collectives, attend(): every_head = lax.all_gather(query, 'tensor', axis=1, tiled=True)  7.27 us
    all_to_all x1, waiting for transfers between devices, local(): lax.all_to_all(outgoing(send_table, value_scales), 'replica', split_axis=...  6.38 us
    all_to_all x1, starting transfers between devices, local(): lax.all_to_all(outgoing(send_table, key_scales), 'replica', split_axis=0,...  5.84 us
    all_to_all x1, starting transfers between devices, local(): lax.all_to_all(outgoing(send_table, value_scales), 'replica', split_axis=...  5.51 us
  transfers between devices with their start and end apart: 6, of which 5 were waited for; matrix products, arithmetic and copies ran while one was open for 23% of the time, Pallas kernels for 0%

commit v1 on v0

v1 whole, which is shorter than its diff:
```python
import functools

import jax
import jax.numpy as jnp
from jax import lax
from jax.experimental import pallas as pl
from jax.experimental.pallas import tpu as pltpu
from jax.sharding import PartitionSpec as P

NEGATIVE = -1e30
EPSILON = 1e-06
LANES = 128
MESH = pl.DeviceIdType.MESH


def kernel(
    replicas,
    shards,
    heads_here,
    group,
    chunks,
    dest_ref,
    slot_ref,
    len_ref,
    gate_ref,
    gain_ref,
    scale_ref,
    hidden_hbm,
    qw_hbm,
    ow_hbm,
    keys_hbm,
    values_hbm,
    mixed_ref,
    new_keys_hbm,
    new_values_hbm,
    new_scale_ref,
    hidden,
    qw,
    ow,
    keys,
    values,
    send_codes,
    recv_keys,
    recv_values,
    send_scale,
    recv_scale,
    placed,
    acc,
    queries,
    part_own,
    part_out,
    part_in,
    stat_own,
    stat_out,
    stat_in,
    attended,
    share_own,
    share_out,
    share_in,
    scale_rows,
    bias,
    load_sem,
    qw_sem,
    ow_sem,
    code_send_sem,
    code_recv_sem,
    scale_send_sem,
    scale_recv_sem,
    query_send_sem,
    query_recv_sem,
    part_send_sem,
    part_recv_sem,
    stat_send_sem,
    stat_recv_sem,
    share_send_sem,
    share_recv_sem,
    out_sem,
):
    here = lax.axis_index("replica")
    rank = lax.axis_index("tensor")
    held, span, _ = keys.shape
    moves = slot_ref.shape[1]
    rows, width = hidden.shape
    drafts = rows // held
    per = min(heads_here, group)
    kv_here = heads_here // per
    tall = per * rows
    deep = qw_hbm.shape[0] // chunks
    high = ow_hbm.shape[0] // chunks
    share = width // shards

    loads = [
        pltpu.make_async_copy(keys_hbm, keys, load_sem.at[0]),
        pltpu.make_async_copy(values_hbm, values, load_sem.at[1]),
        pltpu.make_async_copy(hidden_hbm, hidden, load_sem.at[2]),
    ]
    for load in loads:
        load.start()

    def load_qw(c):
        at = pl.ds(pl.multiple_of(c * deep, deep), deep)
        return pltpu.make_async_copy(qw_hbm.at[at], qw.at[at], qw_sem.at[c])

    def load_ow(c):
        at = pl.ds(pl.multiple_of(c * high, high), high)
        return pltpu.make_async_copy(ow_hbm.at[at], ow.at[at], ow_sem.at[c])

    for c in range(chunks):
        load_qw(c).start()

    far = [lax.rem(here + k, replicas) for k in range(1, replicas)]
    partner = rank + 1 - 2 * lax.rem(rank, 2)
    near = []
    for j in range(1, shards // 2):
        pair = lax.rem(rank // 2 + j, shards // 2) * 2
        near += [pair + lax.rem(rank + c, 2) for c in range(2)]
    arrive_order = [partner] + near
    leave_order = near + [partner]

    barrier = pltpu.get_barrier_semaphore()
    for other in far:
        pl.semaphore_signal(barrier, inc=1, device_id=(other, rank), device_id_type=MESH)
    for other in leave_order:
        pl.semaphore_signal(barrier, inc=1, device_id=(here, other), device_id_type=MESH)

    slots = [slot_ref[0, j] for j in range(moves)]

    def leaving(target):
        found = jnp.int32(0)
        for j in range(moves):
            found = jnp.where(dest_ref[here, j] == target, slots[j], found)
        return found

    loads[0].wait()
    loads[1].wait()
    for other in far:
        slot = leaving(other)
        send_codes[0, other] = keys[slot]
        send_codes[1, other] = values[slot]
        send_scale[other] = jnp.broadcast_to(scale_ref[slot], send_scale.shape[1:])
    recv_codes = (recv_keys, recv_values)
    recv_keys[here] = keys[0]
    recv_values[here] = values[0]
    recv_scale[here] = jnp.broadcast_to(scale_ref[0], send_scale.shape[1:])

    pl.semaphore_wait(barrier, replicas - 1 + shards - 1)

    def move_codes(which, k):
        other = far[k]
        return pltpu.make_async_remote_copy(
            src_ref=send_codes.at[which, other],
            dst_ref=recv_codes[which].at[here],
            send_sem=code_send_sem.at[which, other],
            recv_sem=code_recv_sem.at[which, here],
            device_id=(other, rank),
            device_id_type=MESH,
        )

    def take_codes(which, k):
        other = far[k]
        return pltpu.make_async_remote_copy(
            src_ref=send_codes.at[which, other],
            dst_ref=recv_codes[which].at[other],
            send_sem=code_send_sem.at[which, other],
            recv_sem=code_recv_sem.at[which, other],
            device_id=(other, rank),
            device_id_type=MESH,
        )

    def move_scale(k, at):
        other = far[k]
        return pltpu.make_async_remote_copy(
            src_ref=send_scale.at[other],
            dst_ref=recv_scale.at[at],
            send_sem=scale_send_sem.at[other],
            recv_sem=scale_recv_sem.at[at],
            device_id=(other, rank),
            device_id_type=MESH,
        )

    for which in range(2):
        for k in range(replicas - 1):
            move_codes(which, k).start()
    for k in range(replicas - 1):
        move_scale(k, here).start()

    lane = lax.broadcasted_iota(jnp.int32, (tall, LANES), 1)
    row_request = lax.rem(lax.broadcasted_iota(jnp.int32, (tall, LANES), 0), rows) // drafts
    table = jnp.zeros((tall, LANES), jnp.float32)
    for r in range(held):
        table = jnp.where(row_request == r, scale_ref[r], table)
    scale_rows[...] = table
    wide = held * span
    column = lax.broadcasted_iota(jnp.int32, (tall, wide), 1)
    column_request = column // span
    row_of = lax.rem(lax.broadcasted_iota(jnp.int32, (tall, wide), 0), rows) // drafts
    limit = jnp.zeros((tall, wide), jnp.int32)
    for r in range(held):
        limit = jnp.where(column_request == r, len_ref[r], limit)
    position = rank * span + lax.rem(column, span)
    bias[...] = jnp.where((position < limit) & (row_of == column_request), 0.0, NEGATIVE)

    loads[2].wait()
    acc[...] = jnp.zeros_like(acc)

    @pl.loop(0, chunks)
    def _(c):
        load_qw(c).wait()
        load_ow(c).start()
        at = pl.ds(pl.multiple_of(c * deep, deep), deep)
        acc[...] += jnp.dot(hidden[:, at], qw[at, :], preferred_element_type=jnp.float32)

    for h in range(heads_here):
        at = slice(h * LANES, (h + 1) * LANES)
        head = acc[:, at]
        head = head * lax.rsqrt(jnp.mean(head * head, axis=-1, keepdims=True) + EPSILON)
        queries[rank, :, at] = (head * gain_ref[...] * LANES ** (-0.5)).astype(jnp.bfloat16)

    def swap(source, target, send_sem, recv_sem, other, from_at, to_at):
        return pltpu.make_async_remote_copy(
            src_ref=source.at[from_at],
            dst_ref=target.at[to_at],
            send_sem=send_sem.at[other],
            recv_sem=recv_sem.at[to_at],
            device_id=(here, other),
            device_id_type=MESH,
        )

    def query_copy(other, from_at, to_at):
        return swap(queries, queries, query_send_sem, query_recv_sem, other, from_at, to_at)

    def part_copy(other, to_at):
        return swap(part_out, part_in, part_send_sem, part_recv_sem, other, other, to_at)

    def stat_copy(other, to_at):
        return swap(stat_out, stat_in, stat_send_sem, stat_recv_sem, other, other, to_at)

    def share_copy(other, to_at):
        return swap(share_out, share_in, share_send_sem, share_recv_sem, other, other, to_at)

    for other in leave_order:
        query_copy(other, rank, rank).start()

    def block(owner, i):
        kv = (owner * heads_here + i * per) // group
        at = pl.ds(pl.multiple_of(kv * LANES, LANES), LANES)
        query = jnp.concatenate(
            [
                queries[owner, :, (i * per + h) * LANES : (i * per + h + 1) * LANES]
                for h in range(per)
            ],
            axis=0,
        )
        key = keys[:, :, at].reshape(wide, LANES)
        value = values[:, :, at].reshape(wide, LANES)
        score = lax.dot_general(
            query, key, (((1,), (1,)), ((), ())), preferred_element_type=jnp.float32
        )
        table = scale_rows[...]
        key_scale = jnp.sum(jnp.where(lane == kv, table, 0.0), axis=1, keepdims=True)
        value_at = kv + gain_ref.shape[1] // 2
        value_scale = jnp.sum(jnp.where(lane == value_at, table, 0.0), axis=1, keepdims=True)
        valid = bias[...] == 0.0
        score = jnp.where(valid, score * key_scale, NEGATIVE)
        peak = jnp.max(score, axis=1, keepdims=True)
        weight = jnp.where(valid, jnp.exp(score - peak), 0.0)
        total = jnp.sum(weight, axis=1, keepdims=True)
        out = jnp.dot(weight.astype(jnp.bfloat16), value, preferred_element_type=jnp.float32)
        stat = jnp.where(lane == 0, peak, jnp.where(lane == 1, total, 0.0))
        return out * value_scale, stat

    for i in range(kv_here):
        at = slice(i * tall, (i + 1) * tall)
        part_own[at, :], stat_own[at, :] = block(rank, i)

    for other in arrive_order:
        query_copy(other, rank, other).wait_recv()
        for i in range(kv_here):
            at = slice(i * tall, (i + 1) * tall)
            out, stat = block(other, i)
            part_out[other, at, :] = out.astype(jnp.bfloat16)
            stat_out[other, :, at] = stat.T[:8]
        stat_copy(other, rank).start()
        part_copy(other, rank).start()

    top = stat_own[:, 0:1]
    total = stat_own[:, 1:2]
    summed = part_own[...]
    for other in arrive_order:
        stat_copy(other, other).wait_recv()
        part_copy(other, other).wait_recv()
        stat = stat_in[other].T
        peak = stat[:, 0:1]
        now = jnp.maximum(top, peak)
        left = jnp.exp(top - now)
        right = jnp.exp(peak - now)
        total = total * left + stat[:, 1:2] * right
        summed = summed * left + part_in[other].astype(jnp.float32) * right
        top = now
    merged = (summed / total).astype(jnp.bfloat16)
    for h in range(heads_here):
        attended[:, h * LANES : (h + 1) * LANES] = merged[h * rows : (h + 1) * rows]

    @pl.loop(0, chunks)
    def _(c):
        load_ow(c).wait()

    tile = min(share, 512)

    def terms(owner, j):
        at = pl.ds(pl.multiple_of(owner * share + j * tile, LANES), tile)
        return jnp.dot(attended[...], ow[:, at], preferred_element_type=jnp.float32)

    for other in leave_order:
        for j in range(share // tile):
            share_out[other, :, j * tile : (j + 1) * tile] = terms(other, j).astype(jnp.bfloat16)
        share_copy(other, rank).start()
    for j in range(share // tile):
        share_own[:, j * tile : (j + 1) * tile] = terms(rank, j)

    stored = []
    sources = []
    for j in range(moves):
        source = jnp.int32(0)
        for s in range(replicas):
            source = jnp.where(dest_ref[s, j] == here, s, source)
        sources.append(source)
    plan = []
    for r in range(held):
        source = here
        for j in range(moves):
            source = jnp.where(slots[j] == r, sources[j], source)
        plan.append(source)

    def place(which, old, new_hbm):
        for k in range(replicas - 1):
            take_codes(which, k).wait_recv()
        for r in range(held):
            placed[which, r] = jnp.where(plan[r] == here, old[r], recv_codes[which][plan[r]])
        out = pltpu.make_async_copy(placed.at[which], new_hbm, out_sem.at[which])
        out.start()
        stored.append(out)

    place(0, keys, new_keys_hbm)

    total = share_own[...]
    for other in arrive_order:
        share_copy(other, other).wait_recv()
        total = total + share_in[other].astype(jnp.float32)
    gate = jnp.tanh(jnp.full((1, LANES), gate_ref[0], jnp.float32))[:, 0:1]
    at = pl.ds(pl.multiple_of(rank * share, LANES), share)
    mixed_ref[...] = (hidden[:, at].astype(jnp.float32) + gate * total).astype(jnp.bfloat16)

    place(1, values, new_values_hbm)
    for k in range(replicas - 1):
        move_scale(k, far[k]).wait_recv()
    for r in range(held):
        new_scale_ref[r] = jnp.where(
            plan[r] == here, scale_ref[r], recv_scale[plan[r]][0:1]
        )

    for k in range(replicas - 1):
        move_codes(0, k).wait_send()
        move_codes(1, k).wait_send()
        move_scale(k, here).wait_send()
    for other in leave_order:
        query_copy(other, rank, rank).wait_send()
        stat_copy(other, rank).wait_send()
        part_copy(other, rank).wait_send()
        share_copy(other, rank).wait_send()
    for out in stored:
        out.wait()


def local(
    replicas,
    shards,
    hidden,
    q_weight,
    q_gain,
    o_weight,
    attn_gate,
    key_codes,
    value_codes,
    key_scales,
    value_scales,
    lengths,
    dest_replica,
    move_slot,
):
    held, span, kv_width = key_codes.shape
    kv_heads = key_scales.shape[2]
    rows, width = hidden.shape
    out_width = q_weight.shape[1]
    heads_here = out_width // LANES
    group = heads_here * shards // kv_heads
    tall = heads_here * rows
    short = min(heads_here, group) * rows
    chunks = 16
    half = LANES // 2
    share = width // shards
    scales = jnp.concatenate(
        [
            jnp.pad(s.astype(jnp.float32), ((0, 0), (0, 0), (0, half - kv_heads)))
            for s in (key_scales, value_scales)
        ],
        axis=2,
    )
    vmem = pl.BlockSpec(memory_space=pltpu.VMEM)
    smem = pl.BlockSpec(memory_space=pltpu.SMEM)
    anywhere = pl.BlockSpec(memory_space=pl.ANY)
    bf16, f32 = jnp.bfloat16, jnp.float32
    dma = pltpu.SemaphoreType.DMA
    mixed, new_keys, new_values, new_scales = pl.pallas_call(
        functools.partial(kernel, replicas, shards, heads_here, group, chunks),
        out_shape=(
            jax.ShapeDtypeStruct((rows, share), bf16),
            jax.ShapeDtypeStruct(key_codes.shape, bf16),
            jax.ShapeDtypeStruct(key_codes.shape, bf16),
            jax.ShapeDtypeStruct(scales.shape, f32),
        ),
        in_specs=[smem] * 4 + [vmem] * 2 + [anywhere] * 5,
        out_specs=(vmem, anywhere, anywhere, vmem),
        scratch_shapes=[
            pltpu.VMEM(hidden.shape, bf16),
            pltpu.VMEM(q_weight.shape, bf16),
            pltpu.VMEM(o_weight.shape, bf16),
            pltpu.VMEM(key_codes.shape, bf16),
            pltpu.VMEM(key_codes.shape, bf16),
            pltpu.VMEM((2, replicas, span, kv_width), bf16),
            pltpu.VMEM((replicas, span, kv_width), bf16),
            pltpu.VMEM((replicas, span, kv_width), bf16),
            pltpu.VMEM((replicas, 8, LANES), f32),
            pltpu.VMEM((replicas, 8, LANES), f32),
            pltpu.VMEM((2,) + key_codes.shape, bf16),
            pltpu.VMEM((rows, out_width), f32),
            pltpu.VMEM((shards, rows, out_width), bf16),
            pltpu.VMEM((tall, LANES), f32),
            pltpu.VMEM((shards, tall, LANES), bf16),
            pltpu.VMEM((shards, tall, LANES), bf16),
            pltpu.VMEM((tall, LANES), f32),
            pltpu.VMEM((shards, 8, tall), f32),
            pltpu.VMEM((shards, 8, tall), f32),
            pltpu.VMEM((rows, out_width), bf16),
            pltpu.VMEM((rows, share), f32),
            pltpu.VMEM((shards, rows, share), bf16),
            pltpu.VMEM((shards, rows, share), bf16),
            pltpu.VMEM((short, LANES), f32),
            pltpu.VMEM((short, held * span), f32),
            dma((3,)),
            dma((chunks,)),
            dma((chunks,)),
            dma((2, replicas)),
            dma((2, replicas)),
            dma((replicas,)),
            dma((replicas,)),
            dma((shards,)),
            dma((shards,)),
            dma((shards,)),
            dma((shards,)),
            dma((shards,)),
            dma((shards,)),
            dma((shards,)),
            dma((shards,)),
            dma((2,)),
        ],
        compiler_params=pltpu.CompilerParams(
            collective_id=0, has_side_effects=True, vmem_limit_bytes=60 * 2**20
        ),
    )(
        dest_replica,
        move_slot,
        lengths,
        attn_gate,
        q_gain.reshape(1, LANES),
        scales,
        hidden,
        q_weight,
        o_weight,
        key_codes,
        value_codes,
    )
    new_key_scales = new_scales[:, :, :kv_heads].astype(bf16)
    new_value_scales = new_scales[:, :, half : half + kv_heads].astype(bf16)
    return (mixed, new_keys, new_values, new_key_scales, new_value_scales)


def solution(mesh):
    return jax.shard_map(
        functools.partial(local, mesh.shape["replica"], mesh.shape["tensor"]),
        mesh=mesh,
        in_specs=(
            P("replica", None),
            P(None, "tensor"),
            P(),
            P("tensor", None),
            P(),
            P("replica", "tensor", None),
            P("replica", "tensor", None),
            P("replica", "tensor", None),
            P("replica", "tensor", None),
            P("replica"),
            P(),
            P("replica", None),
        ),
        out_specs=(
            P("replica", "tensor"),
            P("replica", "tensor", None),
            P("replica", "tensor", None),
            P("replica", "tensor", None),
            P("replica", "tensor", None),
        ),
        check_vma=False,
    )
```

time: 119 us -> 47.7 us (0.40)
  Pallas kernels: 0 us -> 36.8 us
  waiting for transfers between devices: 23.9 us -> 0 us
  matrix products: 22.6 us -> 0 us
  starting transfers between devices: 18.6 us -> 0 us
  blocking collectives: 18.5 us -> 0 us
  between operations: 15.1 us -> 1.29 us
  other arithmetic: 8.61 us -> 1.35 us
  local copies, waits for them, and re-layouts: 10.5 us -> 7.92 us
    pallas_call x0 -> x1, Pallas kernels: none -> 36.8 us  [local(): pl.pallas_call(functools.partial(kernel, replicas, shards, heads_here, gr...]
    dot_general x12 -> x0, matrix products: 22.6 us -> none  [the longest x1 9.73 us: attend(): terms = jnp.dot(attended, o_weight, preferred_element_type=jnp.float32)]
    all_gather x3 -> x0, blocking collectives: 18.5 us -> none  [the longest x2 11.3 us: merged(): everything = jax.tree.map(lambda part: lax.all_gather(part, axis), array)]
    all_to_all x4 -> x0, starting transfers between devices: 18.5 us -> none  [the longest x1 5.84 us: local(): lax.all_to_all(outgoing(send_table, key_scales), 'replica', split_axis=0,...]
    all_to_all x4 -> x0, waiting for transfers between devices: 18.3 us -> none  [the longest x1 9.74 us: local(): lax.all_to_all(outgoing(send_table, value_codes), 'replica', split_axis=0...]
    add x7 -> x0, other arithmetic: 4.71 us -> none  [the longest x3 4.63 us: softmax_merge(): summed = first[2] * left[..., None] + second[2] * right[..., None]]
    reshape x6 -> x0, local copies, waits for them, and re-layouts: 3.44 us -> none  [the longest x4 3.37 us: outgoing(): moved.astype(jnp.bfloat16).reshape((send_table.shape[0],) + codes.shape[1:])]
    all_gather x1 -> x0, waiting for transfers between devices: 3.2 us -> none  [merged(): everything = jax.tree.map(lambda part: lax.all_gather(part, axis), array)]
  transfers between devices with their start and end apart: 6 -> 0, of which waited for: 5 -> 0; matrix products, arithmetic and copies ran while one was open for 23% -> 0% of each run, Pallas kernels for 0% -> 0%
where the time goes in v1:
time: 47.7 us; the launch traced here: 47.4 us
  Pallas kernels  36.8 us (77%)
  local copies, waits for them, and re-layouts  7.92 us (17%)
  other arithmetic  1.35 us (3%)
  between operations  1.29 us (3%)
    pallas_call x1, Pallas kernels, local(): pl.pallas_call(functools.partial(kernel, replicas, shards, heads_here, gr...  36.8 us
    unnamed x7, local copies, waits for them, and re-layouts  7.84 us

profile of v1, /device:TPU:0, one launch (start us, length us, event | category | flops | bytes accessed | tf_op | source)
XLA Modules:
  0.0 47.4 jit_solution(11298810675967975134)
XLA Ops:
  1.3 0.7 %copy.17 = bf16[8,1,8]{2,1,0:T(2,128)(2,1)S(1)} copy(bf16[8,1,8]{2,0,1:T(8,128)(2,1)} %param.19) | data formatting | bytes 256 | tf_op args[7]
  2.0 0.7 %copy.18 = bf16[8,1,8]{2,1,0:T(2,128)(2,1)S(1)} copy(bf16[8,1,8]{2,0,1:T(8,128)(2,1)} %param.20) | data formatting | bytes 256 | tf_op args[8]
  2.7 0.7 %fusion.1.scale_ref = f32[8,1,128]{2,1,0:T(1,128)} fusion(bf16[8,1,8]{2,1,0:T(2,128)(2,1)S(1)} %copy.18, bf16[8,1,8]{2,1,0:T(2,128)(2,1)S(1)} %copy.17), kind=kLoop, calls=%fused_computation.3 | loop fusion | flops 8192 | bytes 4352 | tf_op jit(solution)/shard_map/concatenate | solution.py:402
  3.3 36.8 %shard_map.155 = (bf16[32,2048]{1,0:T(8,128)(2,1)}, bf16[8,32,1024]{2,1,0:T(8,128)(2,1)}, bf16[8,32,1024]{2,1,0:T(8,128)(2,1)}, f32[8,1,128]{2,1,0:T(1,128)}) custom-call(s32[8,6]{1,0:T(8,128)} %dest_ref.1, s32[1,6]{1,0:T(1,128)} %slot_ref.1, s32[8]{0:T(128)} %len_ref.1, f32[1]{0:T(128)S(6)} %copy.24.gate_ref, f32[1,128]{1,0:T(1,128)} %bitcast.1, ...), custom_call_target="tpu_custom_call" | custom-call | tf_op jit(solution)/shard_map/pallas_call | solution.py:414
  40.1 0.7 %convert.9 = bf16[8,1,128]{2,1,0:T(2,128)(2,1)S(1)} convert(f32[8,1,128]{2,1,0:T(1,128)} %get-tuple-element.12) | non-fusion elementwise | flops 1024 | bytes 6144 | tf_op jit(solution)/shard_map/convert.6
  40.8 0.1 fusion.2
  40.9 0.6 %copy.20 = bf16[8,1,8]{2,0,1:T(8,128)(2,1)} copy(bf16[8,1,8]{2,1,0:T(2,128)(2,1)S(1)} %get-tuple-element.18) | data formatting | bytes 256
  41.5 0.6 %copy.19 = bf16[8,1,8]{2,0,1:T(8,128)(2,1)} copy(bf16[8,1,8]{2,1,0:T(2,128)(2,1)S(1)} %get-tuple-element.19) | data formatting | bytes 256
  42.1 1.6 %copy.25 = bf16[32,2048]{1,0:T(8,128)(2,1)} copy(bf16[32,2048]{1,0:T(8,128)(2,1)} %get-tuple-element.25) | data formatting | bytes 262144
  43.6 1.9 %copy.26 = bf16[8,32,1024]{2,1,0:T(8,128)(2,1)} copy(bf16[8,32,1024]{2,1,0:T(8,128)(2,1)} %get-tuple-element.26) | data formatting | bytes 1048576
  45.5 1.9 %copy.27 = bf16[8,32,1024]{2,1,0:T(8,128)(2,1)} copy(bf16[8,32,1024]{2,1,0:T(8,128)(2,1)} %get-tuple-element.27) | data formatting | bytes 1048576

commit v2 on v1

--- a/solution.py
+++ b/solution.py
@@ -24,16 +24,18 @@
     len_ref,
     gate_ref,
     gain_ref,
-    scale_ref,
+    key_scale_ref,
+    value_scale_ref,
     hidden_hbm,
     qw_hbm,
     ow_hbm,
     keys_hbm,
     values_hbm,
     mixed_ref,
-    new_keys_hbm,
-    new_values_hbm,
-    new_scale_ref,
+    new_keys,
+    new_values,
+    new_key_scale_ref,
+    new_value_scale_ref,
     hidden,
     qw,
     ow,
@@ -44,7 +46,8 @@
     recv_values,
     send_scale,
     recv_scale,
-    placed,
+    scale_ref,
+    scale_out,
     acc,
     queries,
     part_own,
@@ -57,7 +60,8 @@
     share_own,
     share_out,
     share_in,
-    scale_rows,
+    key_rows,
+    value_rows,
     bias,
     load_sem,
     qw_sem,
@@ -74,7 +78,6 @@
     stat_recv_sem,
     share_send_sem,
     share_recv_sem,
-    out_sem,
 ):
     here = lax.axis_index("replica")
     rank = lax.axis_index("tensor")
@@ -131,17 +134,24 @@
             found = jnp.where(dest_ref[here, j] == target, slots[j], found)
         return found
 
+    kv_heads = key_scale_ref.shape[1]
+    scale_ref[...] = jnp.zeros_like(scale_ref)
+    for which, ref in enumerate((key_scale_ref, value_scale_ref)):
+        whole = ref[...].astype(jnp.float32)
+        for r in range(held):
+            scale_ref[r, which : which + 1, 0:kv_heads] = whole[r : r + 1]
+
     loads[0].wait()
     loads[1].wait()
     for other in far:
         slot = leaving(other)
         send_codes[0, other] = keys[slot]
         send_codes[1, other] = values[slot]
-        send_scale[other] = jnp.broadcast_to(scale_ref[slot], send_scale.shape[1:])
+        send_scale[other] = scale_ref[slot]
     recv_codes = (recv_keys, recv_values)
     recv_keys[here] = keys[0]
     recv_values[here] = values[0]
-    recv_scale[here] = jnp.broadcast_to(scale_ref[0], send_scale.shape[1:])
+    recv_scale[here] = scale_ref[0]
 
     pl.semaphore_wait(barrier, replicas - 1 + shards - 1)
 
@@ -186,10 +196,11 @@
 
     lane = lax.broadcasted_iota(jnp.int32, (tall, LANES), 1)
     row_request = lax.rem(lax.broadcasted_iota(jnp.int32, (tall, LANES), 0), rows) // drafts
-    table = jnp.zeros((tall, LANES), jnp.float32)
-    for r in range(held):
-        table = jnp.where(row_request == r, scale_ref[r], table)
-    scale_rows[...] = table
+    for which, scale_rows in enumerate((key_rows, value_rows)):
+        table = jnp.zeros((tall, LANES), jnp.float32)
+        for r in range(held):
+            table = jnp.where(row_request == r, scale_ref[r, which : which + 1], table)
+        scale_rows[...] = table
     wide = held * span
     column = lax.broadcasted_iota(jnp.int32, (tall, wide), 1)
     column_request = column // span
@@ -256,10 +267,9 @@
         score = lax.dot_general(
             query, key, (((1,), (1,)), ((), ())), preferred_element_type=jnp.float32
         )
-        table = scale_rows[...]
-        key_scale = jnp.sum(jnp.where(lane == kv, table, 0.0), axis=1, keepdims=True)
-        value_at = kv + gain_ref.shape[1] // 2
-        value_scale = jnp.sum(jnp.where(lane == value_at, table, 0.0), axis=1, keepdims=True)
+        chosen = lane == kv
+        key_scale = jnp.sum(jnp.where(chosen, key_rows[...], 0.0), axis=1, keepdims=True)
+        value_scale = jnp.sum(jnp.where(chosen, value_rows[...], 0.0), axis=1, keepdims=True)
         valid = bias[...] == 0.0
         score = jnp.where(valid, score * key_scale, NEGATIVE)
         peak = jnp.max(score, axis=1, keepdims=True)
@@ -318,7 +328,6 @@
     for j in range(share // tile):
         share_own[:, j * tile : (j + 1) * tile] = terms(rank, j)
 
-    stored = []
     sources = []
     for j in range(moves):
         source = jnp.int32(0)
@@ -332,16 +341,13 @@
             source = jnp.where(slots[j] == r, sources[j], source)
         plan.append(source)
 
-    def place(which, old, new_hbm):
+    def place(which, old, new):
         for k in range(replicas - 1):
             take_codes(which, k).wait_recv()
         for r in range(held):
-            placed[which, r] = jnp.where(plan[r] == here, old[r], recv_codes[which][plan[r]])
-        out = pltpu.make_async_copy(placed.at[which], new_hbm, out_sem.at[which])
-        out.start()
-        stored.append(out)
-
-    place(0, keys, new_keys_hbm)
+            new[r] = jnp.where(plan[r] == here, old[r], recv_codes[which][plan[r]])
+
+    place(0, keys, new_keys)
 
     total = share_own[...]
     for other in arrive_order:
@@ -351,13 +357,15 @@
     at = pl.ds(pl.multiple_of(rank * share, LANES), share)
     mixed_ref[...] = (hidden[:, at].astype(jnp.float32) + gate * total).astype(jnp.bfloat16)
 
-    place(1, values, new_values_hbm)
+    place(1, values, new_values)
     for k in range(replicas - 1):
         move_scale(k, far[k]).wait_recv()
     for r in range(held):
-        new_scale_ref[r] = jnp.where(
-            plan[r] == here, scale_ref[r], recv_scale[plan[r]][0:1]
-        )
+        row = jnp.where(plan[r] == here, scale_ref[r], recv_scale[plan[r]])
+        scale_out[0, r : r + 1] = row[0:1]
+        scale_out[1, r : r + 1] = row[1:2]
+    new_key_scale_ref[...] = scale_out[0][:, :kv_heads].astype(jnp.bfloat16)
+    new_value_scale_ref[...] = scale_out[1][:, :kv_heads].astype(jnp.bfloat16)
 
     for k in range(replicas - 1):
         move_codes(0, k).wait_send()
@@ -368,8 +376,18 @@
         stat_copy(other, rank).wait_send()
         part_copy(other, rank).wait_send()
         share_copy(other, rank).wait_send()
-    for out in stored:
-        out.wait()
+
+
+def store_out(*refs):
+    count = (len(refs) - 1) // 2
+    sem = refs[-1]
+    copies = [
+        pltpu.make_async_copy(refs[i], refs[count + i], sem.at[i]) for i in range(count)
+    ]
+    for copy in copies:
+        copy.start()
+    for copy in copies:
+        copy.wait()
 
 
 def local(
@@ -397,30 +415,24 @@
     tall = heads_here * rows
     short = min(heads_here, group) * rows
     chunks = 16
-    half = LANES // 2
     share = width // shards
-    scales = jnp.concatenate(
-        [
-            jnp.pad(s.astype(jnp.float32), ((0, 0), (0, 0), (0, half - kv_heads)))
-            for s in (key_scales, value_scales)
-        ],
-        axis=2,
-    )
     vmem = pl.BlockSpec(memory_space=pltpu.VMEM)
     smem = pl.BlockSpec(memory_space=pltpu.SMEM)
     anywhere = pl.BlockSpec(memory_space=pl.ANY)
     bf16, f32 = jnp.bfloat16, jnp.float32
     dma = pltpu.SemaphoreType.DMA
-    mixed, new_keys, new_values, new_scales = pl.pallas_call(
+    results = (
+        ((rows, share), bf16),
+        (key_codes.shape, bf16),
+        (key_codes.shape, bf16),
+        ((held, kv_heads), bf16),
+        ((held, kv_heads), bf16),
+    )
+    staged = pl.pallas_call(
         functools.partial(kernel, replicas, shards, heads_here, group, chunks),
-        out_shape=(
-            jax.ShapeDtypeStruct((rows, share), bf16),
-            jax.ShapeDtypeStruct(key_codes.shape, bf16),
-            jax.ShapeDtypeStruct(key_codes.shape, bf16),
-            jax.ShapeDtypeStruct(scales.shape, f32),
-        ),
-        in_specs=[smem] * 4 + [vmem] * 2 + [anywhere] * 5,
-        out_specs=(vmem, anywhere, anywhere, vmem),
+        out_shape=tuple(pltpu.VMEM(shape, kind) for shape, kind in results),
+        in_specs=[smem] * 4 + [vmem] * 3 + [anywhere] * 5,
+        out_specs=(vmem,) * 5,
         scratch_shapes=[
             pltpu.VMEM(hidden.shape, bf16),
             pltpu.VMEM(q_weight.shape, bf16),
@@ -432,7 +444,8 @@
             pltpu.VMEM((replicas, span, kv_width), bf16),
             pltpu.VMEM((replicas, 8, LANES), f32),
             pltpu.VMEM((replicas, 8, LANES), f32),
-            pltpu.VMEM((2,) + key_codes.shape, bf16),
+            pltpu.VMEM((held, 8, LANES), f32),
+            pltpu.VMEM((2, held, LANES), f32),
             pltpu.VMEM((rows, out_width), f32),
             pltpu.VMEM((shards, rows, out_width), bf16),
             pltpu.VMEM((tall, LANES), f32),
@@ -446,6 +459,7 @@
             pltpu.VMEM((shards, rows, share), bf16),
             pltpu.VMEM((shards, rows, share), bf16),
             pltpu.VMEM((short, LANES), f32),
+            pltpu.VMEM((short, LANES), f32),
             pltpu.VMEM((short, held * span), f32),
             dma((3,)),
             dma((chunks,)),
@@ -462,7 +476,6 @@
             dma((shards,)),
             dma((shards,)),
             dma((shards,)),
-            dma((2,)),
         ],
         compiler_params=pltpu.CompilerParams(
             collective_id=0, has_side_effects=True, vmem_limit_bytes=60 * 2**20
@@ -473,16 +486,28 @@
         lengths,
         attn_gate,
         q_gain.reshape(1, LANES),
-        scales,
+        key_scales.reshape(held, kv_heads),
+        value_scales.reshape(held, kv_heads),
         hidden,
         q_weight,
         o_weight,
         key_codes,
         value_codes,
     )
-    new_key_scales = new_scales[:, :, :kv_heads].astype(bf16)
-    new_value_scales = new_scales[:, :, half : half + kv_heads].astype(bf16)
-    return (mixed, new_keys, new_values, new_key_scales, new_value_scales)
+    mixed, new_keys, new_values, new_key_scales, new_value_scales = pl.pallas_call(
+        store_out,
+        out_shape=tuple(jax.ShapeDtypeStruct(shape, kind) for shape, kind in results),
+        in_specs=[vmem] * len(results),
+        out_specs=(anywhere,) * len(results),
+        scratch_shapes=[dma((len(results),))],
+    )(*[pltpu.with_memory_space_constraint(x, pltpu.VMEM) for x in staged])
+    return (
+        mixed,
+        new_keys,
+        new_values,
+        new_key_scales.reshape(key_scales.shape),
+        new_value_scales.reshape(value_scales.shape),
+    )
 
 
 def solution(mesh):

time: 47.7 us -> 38.9 us (0.82)
  local copies, waits for them, and re-layouts: 7.92 us -> 0 us
  other arithmetic: 1.35 us -> 0 us
  Pallas kernels: 36.8 us -> 37.4 us
    unnamed x7 -> x0, local copies, waits for them, and re-layouts: 7.84 us -> none
    pallas_call x0 -> x1, Pallas kernels: none -> 1.06 us  [local(): pl.pallas_call(store_out, out_shape=tuple((jax.ShapeDtypeStruct(shape, ki...]
    another operation x1 -> x0, other arithmetic: 0.68 us -> none
    concatenate x1 -> x0, other arithmetic: 0.67 us -> none  [local(): jnp.concatenate([jnp.pad(s.astype(jnp.float32), ((0, 0), (0, 0), (0, half...]
    pallas_call x1, Pallas kernels: 36.8 us -> 36.3 us  [local(): pl.pallas_call(functools.partial(kernel, replicas, shards, heads_here, gr...]
where the time goes in v2:
time: 38.9 us; the launch traced here: 38.7 us
  Pallas kernels  37.4 us (96%)
  between operations  1.29 us (3%)
    pallas_call x1, Pallas kernels, local(): pl.pallas_call(functools.partial(kernel, replicas, shards, heads_here, gr...  36.3 us
    pallas_call x1, Pallas kernels, local(): pl.pallas_call(store_out, out_shape=tuple((jax.ShapeDtypeStruct(shape, ki...  1.06 us

profile of v2, /device:TPU:0, one launch (start us, length us, event | category | flops | bytes accessed | tf_op | source)
XLA Modules:
  0.0 38.7 jit_solution(3857238927886686451)
XLA Ops:
  1.3 36.3 %shard_map.155 = (bf16[32,2048]{1,0:T(8,128)(2,1)S(1)}, bf16[8,32,1024]{2,1,0:T(8,128)(2,1)S(1)}, bf16[8,32,1024]{2,1,0:T(8,128)(2,1)S(1)}, bf16[8,8]{1,0:T(8,128)(2,1)S(1)}, bf16[8,8]{1,0:T(8,128)(2,1)S(1)}) custom-call(s32[8,6]{1,0:T(8,128)} %dest_ref.1, s32[1,6]{1,0:T(1,128)} %slot_ref.1, s32[8]{0:T(128)} %len_ref.1, f32[1]{0:T(128)S(6)} %copy.17.gate_ref, ...), custom_call_target="tpu_custom_call" | custom-call | tf_op jit(solution)/shard_map/pallas_call | solution.py:431
  37.6 1.1 %shard_map.156 = (bf16[32,2048]{1,0:T(8,128)(2,1)}, bf16[8,32,1024]{2,1,0:T(8,128)(2,1)}, bf16[8,32,1024]{2,1,0:T(8,128)(2,1)}, bf16[8,8]{1,0:T(8,128)(2,1)}, bf16[8,8]{1,0:T(8,128)(2,1)}) custom-call(bf16[32,2048]{1,0:T(8,128)(2,1)S(1)} %get-tuple-element.15.refs_0_, bf16[8,32,1024]{2,1,0:T(8,128)(2,1)S(1)} %get-tuple-element.16.refs_1_, ...), custom_call_target="tpu_custom_call" | custom-call | tf_op jit(solution)/shard_map/pallas_call | solution.py:497

commit v3 on v2

--- a/solution.py
+++ b/solution.py
@@ -97,7 +97,7 @@
         pltpu.make_async_copy(values_hbm, values, load_sem.at[1]),
         pltpu.make_async_copy(hidden_hbm, hidden, load_sem.at[2]),
     ]
-    for load in loads:
+    for load in loads[:2]:
         load.start()
 
     def load_qw(c):
@@ -107,9 +107,6 @@
     def load_ow(c):
         at = pl.ds(pl.multiple_of(c * high, high), high)
         return pltpu.make_async_copy(ow_hbm.at[at], ow.at[at], ow_sem.at[c])
-
-    for c in range(chunks):
-        load_qw(c).start()
 
     far = [lax.rem(here + k, replicas) for k in range(1, replicas)]
     partner = rank + 1 - 2 * lax.rem(rank, 2)
@@ -143,6 +140,9 @@
 
     loads[0].wait()
     loads[1].wait()
+    loads[2].start()
+    for c in range(chunks):
+        load_qw(c).start()
     for other in far:
         slot = leaving(other)
         send_codes[0, other] = keys[slot]
@@ -217,9 +217,11 @@
     @pl.loop(0, chunks)
     def _(c):
         load_qw(c).wait()
-        load_ow(c).start()
         at = pl.ds(pl.multiple_of(c * deep, deep), deep)
         acc[...] += jnp.dot(hidden[:, at], qw[at, :], preferred_element_type=jnp.float32)
+
+    for c in range(chunks):
+        load_ow(c).start()
 
     for h in range(heads_here):
         at = slice(h * LANES, (h + 1) * LANES)
@@ -246,8 +248,15 @@
     def stat_copy(other, to_at):
         return swap(stat_out, stat_in, stat_send_sem, stat_recv_sem, other, other, to_at)
 
-    def share_copy(other, to_at):
-        return swap(share_out, share_in, share_send_sem, share_recv_sem, other, other, to_at)
+    def share_copy(other, to_at, j):
+        return pltpu.make_async_remote_copy(
+            src_ref=share_out.at[j, other],
+            dst_ref=share_in.at[j, to_at],
+            send_sem=share_send_sem.at[j, other],
+            recv_sem=share_recv_sem.at[j, to_at],
+            device_id=(here, other),
+            device_id_type=MESH,
+        )
 
     for other in leave_order:
         query_copy(other, rank, rank).start()
@@ -323,8 +332,8 @@
 
     for other in leave_order:
         for j in range(share // tile):
-            share_out[other, :, j * tile : (j + 1) * tile] = terms(other, j).astype(jnp.bfloat16)
-        share_copy(other, rank).start()
+            share_out[j, other] = terms(other, j).astype(jnp.bfloat16)
+            share_copy(other, rank, j).start()
     for j in range(share // tile):
         share_own[:, j * tile : (j + 1) * tile] = terms(rank, j)
 
@@ -351,8 +360,10 @@
 
     total = share_own[...]
     for other in arrive_order:
-        share_copy(other, other).wait_recv()
-        total = total + share_in[other].astype(jnp.float32)
+        for j in range(share // tile):
+            share_copy(other, other, j).wait_recv()
+        arrived = [share_in[j, other].astype(jnp.float32) for j in range(share // tile)]
+        total = total + jnp.concatenate(arrived, axis=1)
     gate = jnp.tanh(jnp.full((1, LANES), gate_ref[0], jnp.float32))[:, 0:1]
     at = pl.ds(pl.multiple_of(rank * share, LANES), share)
     mixed_ref[...] = (hidden[:, at].astype(jnp.float32) + gate * total).astype(jnp.bfloat16)
@@ -375,7 +386,8 @@
         query_copy(other, rank, rank).wait_send()
         stat_copy(other, rank).wait_send()
         part_copy(other, rank).wait_send()
-        share_copy(other, rank).wait_send()
+        for j in range(share // tile):
+            share_copy(other, rank, j).wait_send()
 
 
 def store_out(*refs):
@@ -416,6 +428,7 @@
     short = min(heads_here, group) * rows
     chunks = 16
     share = width // shards
+    tile = min(share, 512)
     vmem = pl.BlockSpec(memory_space=pltpu.VMEM)
     smem = pl.BlockSpec(memory_space=pltpu.SMEM)
     anywhere = pl.BlockSpec(memory_space=pl.ANY)
@@ -456,8 +469,8 @@
             pltpu.VMEM((shards, 8, tall), f32),
             pltpu.VMEM((rows, out_width), bf16),
             pltpu.VMEM((rows, share), f32),
-            pltpu.VMEM((shards, rows, share), bf16),
-            pltpu.VMEM((shards, rows, share), bf16),
+            pltpu.VMEM((share // tile, shards, rows, tile), bf16),
+            pltpu.VMEM((share // tile, shards, rows, tile), bf16),
             pltpu.VMEM((short, LANES), f32),
             pltpu.VMEM((short, LANES), f32),
             pltpu.VMEM((short, held * span), f32),
@@ -474,8 +487,8 @@
             dma((shards,)),
             dma((shards,)),
             dma((shards,)),
-            dma((shards,)),
-            dma((shards,)),
+            dma((share // tile, shards)),
+            dma((share // tile, shards)),
         ],
         compiler_params=pltpu.CompilerParams(
             collective_id=0, has_side_effects=True, vmem_limit_bytes=60 * 2**20

time: 38.9 us -> 35.5 us (0.913)
  Pallas kernels: 37.4 us -> 34 us
    pallas_call x1, Pallas kernels: 36.3 us -> 33 us  [local(): pl.pallas_call(functools.partial(kernel, replicas, shards, heads_here, gr...]
where the time goes in v3:
time: 35.5 us; the launch traced here: 35.3 us
  Pallas kernels  34 us (96%)
  between operations  1.29 us (4%)
    pallas_call x1, Pallas kernels, local(): pl.pallas_call(functools.partial(kernel, replicas, shards, heads_here, gr...  33 us
    pallas_call x1, Pallas kernels, local(): pl.pallas_call(store_out, out_shape=tuple((jax.ShapeDtypeStruct(shape, ki...  1.06 us

profile of v3, /device:TPU:0, one launch (start us, length us, event | category | flops | bytes accessed | tf_op | source)
XLA Modules:
  0.0 35.3 jit_solution(137827282295612222)
XLA Ops:
  1.3 33.0 %shard_map.155 = (bf16[32,2048]{1,0:T(8,128)(2,1)S(1)}, bf16[8,32,1024]{2,1,0:T(8,128)(2,1)S(1)}, bf16[8,32,1024]{2,1,0:T(8,128)(2,1)S(1)}, bf16[8,8]{1,0:T(8,128)(2,1)S(1)}, bf16[8,8]{1,0:T(8,128)(2,1)S(1)}) custom-call(s32[8,6]{1,0:T(8,128)} %dest_ref.1, s32[1,6]{1,0:T(1,128)} %slot_ref.1, s32[8]{0:T(128)} %len_ref.1, f32[1]{0:T(128)S(6)} %copy.17.gate_ref, ...), custom_call_target="tpu_custom_call" | custom-call | tf_op jit(solution)/shard_map/pallas_call | solution.py:444
  34.2 1.1 %shard_map.156 = (bf16[32,2048]{1,0:T(8,128)(2,1)}, bf16[8,32,1024]{2,1,0:T(8,128)(2,1)}, bf16[8,32,1024]{2,1,0:T(8,128)(2,1)}, bf16[8,8]{1,0:T(8,128)(2,1)}, bf16[8,8]{1,0:T(8,128)(2,1)}) custom-call(bf16[32,2048]{1,0:T(8,128)(2,1)S(1)} %get-tuple-element.15.refs_0_, bf16[8,32,1024]{2,1,0:T(8,128)(2,1)S(1)} %get-tuple-element.16.refs_1_, ...), custom_call_target="tpu_custom_call" | custom-call | tf_op jit(solution)/shard_map/pallas_call | solution.py:510
